TPU v7x, 128 devices: a whole 4x4x4 slice. The times are simulated.
128 devices in a mesh: cache: 32 (over x, y, z_lo), batch: 4 (over z_hi, core).
Axes of the slice: x: 4, y: 4, z: 4 (z_hi: 2, z_lo: 2; z = z_hi * 2 + z_lo), core: 2. Of those that a mesh axis runs over, the one named last changes fastest.
Arguments:
- queries: bfloat16 [3, 4096, 768], P(None, 'batch')
- positives: int32 [3, 4096], P(None, 'batch'), may hold values from 0 to 511
- block_list: int32 [3, 32, 192], P(None, 'batch'), may hold values from 0 to 255
- block_count: int32 [3, 32], P(None, 'batch'), may hold values from 1 to 192
- refresh_owner: int32 [3], replicated, may hold values from 0 to 31, as said below
- cache: float32 [32768, 768], P('cache'), may hold values from -6 to 6
- fresh: float32 [16384, 768], P('cache')
Outputs:
- query_grad: float32 [3, 4096, 768], P(None, ('batch', 'cache'))
- cache_grad: float32 [32768, 768], P('cache')
Inputs may be any that keep to these rules, and one draw needn't show every extreme that they name: `refresh_owner`: 3 different owners; owner 0 and owner 32 - 1 are always among them.
All inputs are finite; a program needn't handle non-finite values.
Results may differ from a plain program's by a relative error of at most 0.0003.
Values sent between devices are 32-bit elements; how exact they have to be, the bound alone decides.
A program may use at most 128 MiB of HBM per device.

v0:
```python
import math
import jax
import jax.numpy as jnp
from jax import lax
from jax.sharding import PartitionSpec as P

BLK = 128


def broadcast(block, axis, holder):
    block = jnp.where(lax.axis_index(axis) == holder, block, jnp.zeros_like(block))
    return lax.psum(block, axis)


def on_device(queries, positives, block_list, block_count, refresh_owner, cache, fresh):
    highest = lax.Precision.HIGHEST
    steps, group_rows, width = queries.shape
    cache_rows = cache.shape[0]
    slab_rows = fresh.shape[0]
    owners = lax.axis_size("cache")
    own_index = lax.axis_index("cache")
    share = group_rows // owners
    home_start = own_index * share
    group_blocks = block_list.shape[1]
    list_width = block_list.shape[2]
    own_blocks = cache_rows // BLK
    scale = 2.0 / math.sqrt(width)
    block_ids = own_index * own_blocks + jnp.arange(own_blocks, dtype=jnp.int32)
    current = cache
    grad_total = jnp.zeros((cache_rows, width), jnp.float32)
    results = []
    for step in range(steps):
        owner = refresh_owner[step]
        is_owner = owner == own_index
        refreshed = jnp.concatenate([fresh, current[slab_rows:]], axis=0)
        current = jnp.where(is_owner, refreshed, current)
        valid = jnp.arange(list_width, dtype=jnp.int32)[None, :] < block_count[step][:, None]
        hits = (block_list[step][:, :, None] == block_ids[None, None, :]) & valid[:, :, None]
        member = jnp.any(hits, axis=1)
        mask = jnp.broadcast_to(member[:, None, :, None], (group_blocks, BLK, own_blocks, BLK))
        mask = mask.reshape(group_rows, cache_rows)
        query_rows = queries[step].astype(jnp.float32)
        scores = scale * jnp.dot(query_rows, current.T, precision=highest)
        scores = jnp.where(mask, scores, -1e30)
        peak = jnp.max(scores, axis=1)
        slab = broadcast(fresh, "cache", owner)
        home_queries = lax.dynamic_slice_in_dim(query_rows, home_start, share, 0)
        slab_scores = scale * jnp.dot(home_queries, slab.T, precision=highest)
        filler = jnp.full((group_rows,), -1e30, jnp.float32)
        slab_peak = lax.dynamic_update_slice_in_dim(
            filler, jnp.max(slab_scores, axis=1), home_start, 0
        )
        peak = jnp.maximum(peak, slab_peak)
        top = lax.pmax(peak, "cache")
        total = jnp.sum(jnp.where(mask, jnp.exp(scores - top[:, None]), 0.0), axis=1)
        home_top = lax.dynamic_slice_in_dim(top, home_start, share, 0)
        slab_total = jnp.sum(jnp.exp(slab_scores - home_top[:, None]), axis=1)
        home_part = lax.dynamic_slice_in_dim(total, home_start, share, 0) + slab_total
        total = lax.dynamic_update_slice_in_dim(total, home_part, home_start, 0)
        total = lax.psum(total, "cache")
        lse = top + jnp.log(total)
        probs = jnp.exp(scores - lse[:, None])
        home_lse = lax.dynamic_slice_in_dim(lse, home_start, share, 0)
        slab_probs = jnp.exp(slab_scores - home_lse[:, None])
        home_pos = lax.dynamic_slice_in_dim(positives[step], home_start, share, 0)
        home_term = jnp.dot(slab_probs, slab, precision=highest) - jnp.take(slab, home_pos, axis=0)
        term = jnp.dot(probs, current, precision=highest)
        mine = lax.psum_scatter(term, "cache", scatter_dimension=0, tiled=True)
        mine = mine + home_term
        results.append(mine)
        step_grad = lax.dot_general(probs, query_rows, (((0,), (0,)), ((), ())), precision=highest)
        grad_total = grad_total + lax.psum(step_grad, "batch")
    return (jnp.stack(results, axis=0), grad_total)


def solution(mesh):
    return jax.shard_map(
        on_device,
        mesh=mesh,
        in_specs=(
            P(None, "batch", None),
            P(None, "batch"),
            P(None, "batch", None),
            P(None, "batch"),
            P(),
            P("cache", None),
            P("cache", None),
        ),
        out_specs=(P(None, ("batch", "cache"), None), P("cache", None)),
        check_vma=False,
    )
```

profile of v0, /device:TPU:1, one launch (start us, length us, event | category | flops | bytes accessed | tf_op | source)
XLA Modules:
  0.0 1261.3 jit_solution(4495534913368518108)
XLA Ops:
  10.5 3.7 broadcast_select_fusion.2
  16.5 1.9 copy-done.11
  20.5 1.7 copy-done.4
  23.8 4.8 fusion.60
  29.0 9.3 fusion.65
  38.6 7.3 fusion.67
  47.2 7.4 fusion.63
  54.7 270.4 %all-reduce.8.cloned.1.call-done = (f32[512,768]{1,0:T(8,128)}, f32[512,768]{1,0:T(8,128)}, f32[512,768]{1,0:T(8,128)}) async-done(((f32[512,768]{1,0:T(8,128)}, f32[512,768]{1,0:T(8,128)}, f32[512,768]{1,0:T(8,128)}), (f32[512,768]{1,0:T(8,128)}, f32[512,768]{1,0:T(8,128)}, f32[512,768]{1,0:T(8,128)})) %all-reduce.8.cloned.1.call-update) | async-done | bytes 4718608 | tf_op jit(solution)/shard_map/psum | solution.py:12
  325.1 2.5 fusion.64
  327.9 2.4 fusion.66
  330.5 1.8 fusion.68
  333.0 130.1 %all-reduce.2 = (f32[1024]{0:T(1024)S(1)}, f32[1024]{0:T(1024)S(1)}, f32[1024]{0:T(1024)S(1)}) all-reduce(f32[1024]{0:T(1024)S(1)} %max.17, f32[1024]{0:T(1024)S(1)} %max.16, f32[1024]{0:T(1024)S(1)} %max.15), channel_id=1, replica_groups=mesh['cache'=32,'batch'=4] {'cache'}, use_global_device_ids=true, to_apply=%region_22.24 | all-reduce | flops 3072 | bytes 24576 | tf_op jit(solution)/shard_map/pmax | solution.py:54
  463.2 3.7 select_reduce_fusion
  471.5 124.2 %all-reduce = (f32[1024]{0:T(1024)S(1)}, f32[1024]{0:T(1024)S(1)}, f32[1024]{0:T(1024)S(1)}) all-reduce(f32[1024]{0:T(1024)S(1)} %add_dynamic-update-slice_fusion, f32[1024]{0:T(1024)S(1)} %add_dynamic-update-slice_fusion.1, f32[1024]{0:T(1024)S(1)} %add_dynamic-update-slice_fusion.2), channel_id=1, replica_groups=mesh['cache'=32,'batch'=4] {'cache'}, use_global_device_ids=true, to_apply=%region_25.27 | all-reduce | flops 3072 | bytes 24576 | tf_op jit(solution)/shard_map/psum | solution.py:60
  595.8 14.5 %fusion.5 = f32[1024,768]{1,0:T(8,128)} fusion(f32[1024,1024]{0,1:T(8,128)} %get-tuple-element.40, f32[1024]{0:T(1024)S(1)} %log_add_fusion, f32[1024,768]{1,0:T(8,128)} %copy-done.4, f32[512,768]{1,0:T(8,128)S(1)} %copy-done, f32[512,768]{1,0:T(8,128)S(1)} %copy-done.13, pred[]{:T(512)S(6)} %eq.73), kind=kOutput, calls=%fused_computation.20 | convolution fusion | flops 9666297856 | bytes 13635585 | tf_op jit(solution)/shard_map/dot_general | solution.py:67
  610.4 1.8 copy-done.6
  612.2 13.5 %fusion.3 = f32[1024,768]{1,0:T(8,128)} fusion(f32[1024,768]{1,0:T(8,128)S(1)} %copy-done.6, f32[1024,1024]{0,1:T(8,128)} %get-tuple-element.44, f32[1024]{0:T(1024)S(1)} %log_add_fusion.1), kind=kOutput, calls=%fused_computation.18 | convolution fusion | flops 9664724992 | bytes 10489856 | tf_op jit(solution)/shard_map/dot_general | solution.py:67
  625.8 1.8 copy-done.3
  627.6 13.4 %fusion.1 = f32[1024,768]{1,0:T(8,128)} fusion(f32[1024,768]{1,0:T(8,128)S(1)} %copy-done.3, f32[1024,1024]{0,1:T(8,128)} %get-tuple-element.48, f32[1024]{0:T(1024)S(1)} %log_add_fusion.2), kind=kOutput, calls=%fused_computation.16 | convolution fusion | flops 9664724992 | bytes 10489856 | tf_op jit(solution)/shard_map/dot_general | solution.py:67
  641.1 8.2 fusion
  649.3 7.2 fusion.2
  656.6 8.8 add_add_fusion
  667.1 2.7 gather_fusion.2
  671.6 151.8 %reduce-scatter.8.cloned.1.call-done = f32[32,768]{1,0:T(8,128)} async-done(((f32[1024,768]{1,0:T(8,128)}), f32[32,768]{1,0:T(8,128)}) %reduce-scatter.8.cloned.1.call-update) | async-done | bytes 98320 | tf_op jit(solution)/shard_map/reduce_scatter | solution.py:68
  823.4 2.7 fusion.24
  826.1 162.2 %reduce-scatter.6.cloned.1.call-done = f32[32,768]{1,0:T(8,128)} async-done(((f32[1024,768]{1,0:T(8,128)}), f32[32,768]{1,0:T(8,128)}) %reduce-scatter.6.cloned.1.call-update) | async-done | bytes 98320 | tf_op jit(solution)/shard_map/reduce_scatter | solution.py:68
  988.3 2.6 fusion.26
  990.9 161.3 %reduce-scatter.4.cloned.1.call-done = f32[32,768]{1,0:T(8,128)} async-done(((f32[1024,768]{1,0:T(8,128)}), f32[32,768]{1,0:T(8,128)}) %reduce-scatter.4.cloned.1.call-update) | async-done | bytes 98320 | tf_op jit(solution)/shard_map/reduce_scatter | solution.py:68
  1152.2 1.9 fusion.28
  1154.1 1.6 pad_maximum_fusion.3
  1155.7 95.0 %all-reduce.6.cloned.1.call-done = f32[1024,768]{1,0:T(8,128)} async-done(((f32[1024,768]{1,0:T(8,128)}), f32[1024,768]{1,0:T(8,128)}) %all-reduce.6.cloned.1.call-update) | async-done | bytes 3145744 | tf_op jit(solution)/shard_map/psum | solution.py:72
  1250.7 3.8 copy.31
  (115 shorter events, 16.7 us)
Async XLA Ops:
  7.2 317.9 %all-reduce.8.cloned.1.call-start = ((), (), s32[]{:S(2)}) async-start(), calls=%async_computation.7 | async-start | bytes 9437184 | tf_op jit(solution)/shard_map/psum | solution.py:12
  14.2 2.3 copy-start
  14.2 2.3 slice-start
  14.3 809.2 %reduce-scatter.8.cloned.1.call-start = ((), (), s32[]{:S(2)}) async-start(), calls=%async_computation.5 | async-start | bytes 3244032 | tf_op jit(solution)/shard_map/reduce_scatter | solution.py:68
  16.5 1.9 copy-start.11
  18.8 1.7 copy-start.1
  20.5 1.7 copy-start.4
  22.1 0.8 copy-start.22
  22.2 24.0 %copy-start.12 = (f32[512,768]{1,0:T(8,128)}, f32[512,768]{1,0:T(8,128)S(1)}, u32[]{:S(2)}) copy-start(f32[512,768]{1,0:T(8,128)S(1)} %slice.79) | copy-start | bytes 4718596
  23.8 5.1 copy-start.5
  28.6 10.0 slice-start.1
  28.9 9.3 copy-start.17
  28.9 9.7 copy-start.2
  28.9 9.7 slice-start.2
  38.6 7.3 copy-start.19
  46.3 1.0 copy-start.21
  325.1 5.5 copy-start.8
  332.3 134.6 %copy-start.18 = (pred[8,128,8,128]{1,0,3,2:T(8,128)(4,1)S(1)}, pred[8,128,8,128]{1,0,3,2:T(8,128)(4,1)}, u32[]{:S(2)}) copy-start(pred[8,128,8,128]{1,0,3,2:T(8,128)(4,1)} %copy-done.17) | copy-start | bytes 3145732
  463.1 3.9 copy-start.14
  466.8 2.2 copy-start.16
  466.8 2.5 copy-start.20
  468.1 127.7 %copy-start.13 = (f32[512,768]{1,0:T(8,128)S(1)}, f32[512,768]{1,0:T(8,128)}, u32[]{:S(2)}) copy-start(f32[512,768]{1,0:T(8,128)} %copy-done.12) | copy-start | bytes 4718596
  610.3 1.9 copy-start.6
  610.3 378.0 %reduce-scatter.6.cloned.1.call-start = ((), (), s32[]{:S(2)}) async-start(), calls=%async_computation.4 | async-start | bytes 3244032 | tf_op jit(solution)/shard_map/reduce_scatter | solution.py:68
  625.7 1.9 copy-start.3
  625.8 526.4 %reduce-scatter.4.cloned.1.call-start = ((), (), s32[]{:S(2)}) async-start(), calls=%async_computation.3 | async-start | bytes 3244032 | tf_op jit(solution)/shard_map/reduce_scatter | solution.py:68
  641.0 609.7 %all-reduce.6.cloned.1.call-start = ((), (), s32[]{:S(2)}) async-start(), calls=%async_computation.6 | async-start | bytes 6291456 | tf_op jit(solution)/shard_map/psum | solution.py:72
  641.1 8.2 copy-start.15
  649.3 7.3 copy-start.7
  656.6 8.8 copy-start.23
  665.4 4.4 copy-start.10
  665.4 5.6 copy-start.9
  (1 other events, 0.7 us)
Sparse Core Ops, SparseCore 0:
  14.4 310.6 all-reduce.7
  610.4 212.9 reduce-scatter.7
  826.5 161.7 reduce-scatter.5
  990.6 161.5 reduce-scatter.3
  1154.7 95.9 all-reduce.5
where the time goes:
time: 1260 us
  waiting for transfers between devices  841 us (67%)
  blocking collectives  254 us (20%)
  matrix products  104 us (8%)
  local copies, waits for them, and re-layouts  29.7 us (2%)
  between operations  18.6 us (1%)
  other arithmetic  14.1 us (1%)
    reduce_scatter x3, waiting for transfers between devices, on_device(): mine = lax.psum_scatter(term, 'cache', scatter_dimension=0, tiled=True)  475 us
    psum x1, waiting for transfers between devices, broadcast(): return lax.psum(block, axis)  270 us
    pmax x1, blocking collectives, on_device(): top = lax.pmax(peak, 'cache')  130 us
    psum x1, blocking collectives, on_device(): total = lax.psum(total, 'cache')  124 us
    psum x1, waiting for transfers between devices, on_device(): grad_total = grad_total + lax.psum(step_grad, 'batch')  95 us
    dot_general x3, matrix products, on_device(): term = jnp.dot(probs, current, precision=highest)  41.5 us
  transfers between devices with their start and end apart: 5, of which 5 were waited for; matrix products, arithmetic and copies ran while one was open for 8% of the time, Pallas kernels for 0%

commit v1 on v0

--- a/solution.py
+++ b/solution.py
@@ -1,3 +1,4 @@
+import functools
 import math
 import jax
 import jax.numpy as jnp
@@ -5,6 +6,13 @@
 from jax.sharding import PartitionSpec as P
 
 BLK = 128
+
+
+def number_floor(message, row_axis):
+    return jnp.sum(lax.all_gather(message, row_axis), 0)
+
+
+obtain_the_rails = functools.partial(number_floor, row_axis="batch")
 
 
 def broadcast(block, axis, holder):
@@ -69,7 +77,7 @@
         mine = mine + home_term
         results.append(mine)
         step_grad = lax.dot_general(probs, query_rows, (((0,), (0,)), ((), ())), precision=highest)
-        grad_total = grad_total + lax.psum(step_grad, "batch")
+        grad_total = grad_total + obtain_the_rails(step_grad)
     return (jnp.stack(results, axis=0), grad_total)
 
 

time: 1260 us -> 1460 us (1.16)
  waiting for transfers between devices: 841 us -> 1010 us
  other arithmetic: 14.1 us -> 41.9 us
    all_gather x0 -> x3, waiting for transfers between devices: none -> 266 us  [number_floor(): return jnp.sum(lax.all_gather(message, row_axis), 0)]
    psum x1 -> x0, waiting for transfers between devices: 95 us -> none  [on_device(): grad_total = grad_total + lax.psum(step_grad, 'batch')]
    reduce_sum x0 -> x3, other arithmetic: none -> 20.7 us  [number_floor(): return jnp.sum(lax.all_gather(message, row_axis), 0)]
  transfers between devices with their start and end apart: 5 -> 7, of which waited for: 5 -> 7; matrix products, arithmetic and copies ran while one was open for 8% -> 8% of each run, Pallas kernels for 0% -> 0%
where the time goes in v1:
time: 1460 us; the launch traced here: 1450 us
  waiting for transfers between devices  1010 us (69%)
  blocking collectives  253 us (17%)
  matrix products  110 us (8%)
  other arithmetic  41.9 us (3%)
  local copies, waits for them, and re-layouts  22 us (2%)
  between operations  18.9 us (1%)
    reduce_scatter x3, waiting for transfers between devices, on_device(): mine = lax.psum_scatter(term, 'cache', scatter_dimension=0, tiled=True)  474 us
    psum x1, waiting for transfers between devices, broadcast(): return lax.psum(block, axis)  269 us
    all_gather x3, waiting for transfers between devices, number_floor(): return jnp.sum(lax.all_gather(message, row_axis), 0)  266 us
    pmax x1, blocking collectives, on_device(): top = lax.pmax(peak, 'cache')  128 us
    psum x1, blocking collectives, on_device(): total = lax.psum(total, 'cache')  125 us
    dot_general x3, matrix products, on_device(): term = jnp.dot(probs, current, precision=highest)  42.7 us
  transfers between devices with their start and end apart: 7, of which 7 were waited for; matrix products, arithmetic and copies ran while one was open for 8% of the time, Pallas kernels for 0%

profile of v1, /device:TPU:1, one launch (start us, length us, event | category | flops | bytes accessed | tf_op | source)
XLA Modules:
  0.0 1454.9 jit_solution(7316383097562187674)
XLA Ops:
  10.6 3.7 broadcast_select_fusion.2
  19.1 2.4 fusion.7
  24.1 4.6 fusion.58
  29.1 9.7 fusion.63
  39.2 7.3 fusion.65
  47.9 9.2 fusion.61
  57.1 269.1 %all-reduce.5.cloned.1.call-done = (f32[512,768]{1,0:T(8,128)}, f32[512,768]{1,0:T(8,128)}, f32[512,768]{1,0:T(8,128)}) async-done(((f32[512,768]{1,0:T(8,128)}, f32[512,768]{1,0:T(8,128)}, f32[512,768]{1,0:T(8,128)}), (f32[512,768]{1,0:T(8,128)}, f32[512,768]{1,0:T(8,128)}, f32[512,768]{1,0:T(8,128)})) %all-reduce.5.cloned.1.call-update) | async-done | bytes 4718608 | tf_op jit(solution)/shard_map/psum | solution.py:20
  326.1 2.5 fusion.62
  328.9 2.4 fusion.64
  333.9 128.4 %all-reduce.2 = (f32[1024]{0:T(1024)S(1)}, f32[1024]{0:T(1024)S(1)}, f32[1024]{0:T(1024)S(1)}) all-reduce(f32[1024]{0:T(1024)S(1)} %max.17, f32[1024]{0:T(1024)S(1)} %max.16, f32[1024]{0:T(1024)S(1)} %max.15), channel_id=1, replica_groups=mesh['cache'=32,'batch'=4] {'cache'}, use_global_device_ids=true, to_apply=%region_22.24 | all-reduce | flops 3072 | bytes 24576 | tf_op jit(solution)/shard_map/pmax | solution.py:62
  462.3 3.7 select_reduce_fusion
  470.7 124.6 %all-reduce = (f32[1024]{0:T(1024)S(1)}, f32[1024]{0:T(1024)S(1)}, f32[1024]{0:T(1024)S(1)}) all-reduce(f32[1024]{0:T(1024)S(1)} %add_dynamic-update-slice_fusion, f32[1024]{0:T(1024)S(1)} %add_dynamic-update-slice_fusion.1, f32[1024]{0:T(1024)S(1)} %add_dynamic-update-slice_fusion.2), channel_id=1, replica_groups=mesh['cache'=32,'batch'=4] {'cache'}, use_global_device_ids=true, to_apply=%region_25.27 | all-reduce | flops 3072 | bytes 24576 | tf_op jit(solution)/shard_map/psum | solution.py:68
  595.3 14.5 fusion.5
  609.9 14.8 %fusion.3 = f32[1024,768]{1,0:T(8,128)} fusion(f32[1024,768]{1,0:T(8,128)} %fusion.7, f32[1024,1024]{0,1:T(8,128)} %get-tuple-element.44, f32[1024]{0:T(1024)S(1)} %log_add_fusion.1), kind=kOutput, calls=%fused_computation.18 | convolution fusion | flops 9664724992 | bytes 10489856 | tf_op jit(solution)/shard_map/dot_general | solution.py:75
  626.6 13.4 fusion.1
  640.1 9.2 fusion.4
  649.3 9.0 fusion
  658.4 9.0 fusion.2
  669.0 2.7 gather_fusion.2
  673.6 148.3 %reduce-scatter.8.cloned.1.call-done = f32[32,768]{1,0:T(8,128)} async-done(((f32[1024,768]{1,0:T(8,128)}), f32[32,768]{1,0:T(8,128)}) %reduce-scatter.8.cloned.1.call-update) | async-done | bytes 98320 | tf_op jit(solution)/shard_map/reduce_scatter | solution.py:76
  821.9 2.4 fusion.22
  824.3 163.4 %reduce-scatter.6.cloned.1.call-done = f32[32,768]{1,0:T(8,128)} async-done(((f32[1024,768]{1,0:T(8,128)}), f32[32,768]{1,0:T(8,128)}) %reduce-scatter.6.cloned.1.call-update) | async-done | bytes 98320 | tf_op jit(solution)/shard_map/reduce_scatter | solution.py:76
  987.8 2.6 fusion.24
  990.4 162.3 %reduce-scatter.4.cloned.1.call-done = f32[32,768]{1,0:T(8,128)} async-done(((f32[1024,768]{1,0:T(8,128)}), f32[32,768]{1,0:T(8,128)}) %reduce-scatter.4.cloned.1.call-update) | async-done | bytes 98320 | tf_op jit(solution)/shard_map/reduce_scatter | solution.py:76
  1152.7 1.9 fusion.26
  1156.2 104.6 %all-gather.11.cloned.1.call-done = f32[4096,768]{1,0:T(8,128)} async-done(((f32[1024,768]{1,0:T(8,128)}), f32[4096,768]{1,0:T(8,128)}) %all-gather.11.cloned.1.call-update) | async-done | bytes 12582928 | tf_op jit(solution)/shard_map/all_gather | solution.py:12
  1260.8 5.8 reduce_sum.89
  1266.6 81.4 %all-gather.7.cloned.1.call-done = f32[4096,768]{1,0:T(8,128)} async-done(((f32[1024,768]{1,0:T(8,128)}), f32[4096,768]{1,0:T(8,128)}) %all-gather.7.cloned.1.call-update) | async-done | bytes 12582928 | tf_op jit(solution)/shard_map/all_gather | solution.py:12
  1348.0 7.5 reduce_sum.87
  1355.5 79.8 %all-gather.9.cloned.1.call-done = f32[4096,768]{1,0:T(8,128)} async-done(((f32[1024,768]{1,0:T(8,128)}), f32[4096,768]{1,0:T(8,128)}) %all-gather.9.cloned.1.call-update) | async-done | bytes 12582928 | tf_op jit(solution)/shard_map/all_gather | solution.py:12
  1435.3 7.5 reduce_sum.88
  1442.8 5.1 add_add_fusion
  (114 shorter events, 23.2 us)
Async XLA Ops:
  7.2 319.0 %all-reduce.5.cloned.1.call-start = ((), (), s32[]{:S(2)}) async-start(), calls=%async_computation.9 | async-start | bytes 9437184 | tf_op jit(solution)/shard_map/psum | solution.py:20
  14.3 2.3 copy-start
  14.3 2.3 slice-start
  14.4 807.5 %reduce-scatter.8.cloned.1.call-start = ((), (), s32[]{:S(2)}) async-start(), calls=%async_computation.5 | async-start | bytes 3244032 | tf_op jit(solution)/shard_map/reduce_scatter | solution.py:76
  16.6 1.9 copy-start.7
  18.9 2.6 copy-start.1
  21.6 1.6 copy-start.19
  21.6 1.7 copy-start.17
  23.1 23.8 %copy-start.8 = (f32[512,768]{1,0:T(8,128)}, f32[512,768]{1,0:T(8,128)S(1)}, u32[]{:S(2)}) copy-start(f32[512,768]{1,0:T(8,128)S(1)} %slice.79) | copy-start | bytes 4718596
  28.7 10.4 slice-start.1
  29.1 9.7 copy-start.12
  29.1 10.1 copy-start.2
  29.1 10.1 slice-start.2
  39.2 7.3 copy-start.14
  46.8 1.0 copy-start.16
  326.1 5.5 copy-start.4
  333.4 132.7 %copy-start.13 = (pred[8,128,8,128]{1,0,3,2:T(8,128)(4,1)S(1)}, pred[8,128,8,128]{1,0,3,2:T(8,128)(4,1)}, u32[]{:S(2)}) copy-start(pred[8,128,8,128]{1,0,3,2:T(8,128)(4,1)} %copy-done.12) | copy-start | bytes 3145732
  462.3 3.9 copy-start.10
  466.0 2.2 copy-start.11
  466.0 2.5 copy-start.15
  467.3 128.1 %copy-start.9 = (f32[512,768]{1,0:T(8,128)S(1)}, f32[512,768]{1,0:T(8,128)}, u32[]{:S(2)}) copy-start(f32[512,768]{1,0:T(8,128)} %copy-done.8) | copy-start | bytes 4718596
  609.9 377.9 %reduce-scatter.6.cloned.1.call-start = ((), (), s32[]{:S(2)}) async-start(), calls=%async_computation.4 | async-start | bytes 3244032 | tf_op jit(solution)/shard_map/reduce_scatter | solution.py:76
  624.7 1.9 copy-start.3
  624.7 527.9 %reduce-scatter.4.cloned.1.call-start = ((), (), s32[]{:S(2)}) async-start(), calls=%async_computation.3 | async-start | bytes 3244032 | tf_op jit(solution)/shard_map/reduce_scatter | solution.py:76
  640.0 620.8 %all-gather.11.cloned.1.call-start = ((), (), s32[]{:S(2)}) async-start(), calls=%async_computation.8 | async-start | bytes 15728640 | tf_op jit(solution)/shard_map/all_gather | solution.py:12
  649.3 698.7 %all-gather.7.cloned.1.call-start = ((), (), s32[]{:S(2)}) async-start(), calls=%async_computation.6 | async-start | bytes 15728640 | tf_op jit(solution)/shard_map/all_gather | solution.py:12
  658.4 776.9 %all-gather.9.cloned.1.call-start = ((), (), s32[]{:S(2)}) async-start(), calls=%async_computation.7 | async-start | bytes 15728640 | tf_op jit(solution)/shard_map/all_gather | solution.py:12
  658.4 9.1 copy-start.18
  667.5 4.3 copy-start.6
  667.5 5.5 copy-start.5
Sparse Core Ops, SparseCore 0:
  14.5 311.6 all-reduce.4
  610.0 211.8 reduce-scatter.7
  824.4 163.3 reduce-scatter.5
  990.6 162.0 reduce-scatter.3
  1154.3 106.5 all-gather.10
  1262.5 85.4 all-gather.6
  1349.8 85.4 all-gather.8
